TPU v7x, 512 devices: a whole 4x8x8 slice. The times are simulated.
512 devices in a mesh: pipe: 8 (over y_lo, core), tensor: 64 (over y_hi, x, z).
Axes of the slice: x: 4, y: 8 (y_hi: 2, y_lo: 4; y = y_hi * 4 + y_lo), z: 8, core: 2. Of those that a mesh axis runs over, the one named last changes fastest.
Arguments:
- output_gradient: bfloat16 [8, 64, 2, 64, 1024], P('pipe', 'tensor'), may hold values from -6 to 6
- forward_input: bfloat16 [8, 2, 512, 8192], P('pipe', None, None, 'tensor'), may hold values from -6 to 6
- saved_rank_outputs: bfloat16 [8, 2, 512, 64], P('pipe', None, 'tensor'), may hold values from -6 to 6
- projection_weight: bfloat16 [8, 64, 1024, 1024], P('pipe', 'tensor'), may hold values from -0.0625 to 0.0625
- adapter_down_maps: bfloat16 [8, 8, 64, 8192], P('pipe', None, None, 'tensor'), may hold values from -0.75 to 0.75
- adapter_up_maps: bfloat16 [8, 64, 8, 8, 1024], P('pipe', 'tensor'), may hold values from -0.0625 to 0.0625
- segment_adapter_class: int32 [8, 2, 4], P('pipe'), may hold values from 0 to 7
- live_segment_table: int32 [8, 2], P('pipe'), may hold values from 1 to 4, as said below
Outputs:
- grad_prev: bfloat16 [8, 2, 512, 8192], P('pipe', None, None, 'tensor')
- down_map_gradient: bfloat16 [8, 8, 64, 8192], P('pipe', None, None, 'tensor')
- up_map_gradient: bfloat16 [8, 64, 8, 8, 1024], P('pipe', 'tensor')
Inputs may be any that keep to these rules, and one draw needn't show every extreme that they name: The first live_segment_table segments of a microbatch are live; some microbatch has all 4 live.
All inputs are finite; a program needn't handle non-finite values.
Results may differ from a plain program's by a relative error of at most 0.0049.
Values may be sent and summed in bfloat16 or wider, within the bound.
A program may use at most 64 MiB of HBM per device.

v0:
```python
import jax
import jax.numpy as jnp
from jax import lax
from jax.sharding import PartitionSpec as P

SEG = 128


def partner(value, axis, apart):
    mask = 2**apart
    pairs = [(source, source ^ mask) for source in range(lax.axis_size(axis))]
    return lax.ppermute(value, axis, pairs)


def shifted(block, axis, distance):
    devices = range(lax.axis_size(axis))
    route = [((i - distance) % len(devices), i) for i in devices]
    return lax.ppermute(block, axis, route)


def choose_segment_rows(class_indicator, segment_lookup):
    return jnp.einsum(
        "pzw,wlq->pzlq", class_indicator, segment_lookup, preferred_element_type=jnp.float32
    ).astype(jnp.bfloat16)


def shards(
    output_gradient,
    forward_input,
    saved_rank_outputs,
    projection_weight,
    adapter_down_maps,
    adapter_up_maps,
    segment_adapter_class,
    live_segment_table,
):
    grad_tile = output_gradient[0, 0]
    micro_count, tile_rows, tile_cols = grad_tile.shape
    weight = projection_weight[0, 0]
    up_matrix_tile = adapter_up_maps[0, 0]
    rank_part = up_matrix_tile.shape[1]
    rank_extent = adapter_down_maps.shape[2]
    local_portion = adapter_down_maps.shape[3]
    group_size = lax.axis_size("tensor")
    total_bits = group_size.bit_length() - 1
    low_size = min(group_size, 8)
    low_bits = low_size.bit_length() - 1
    high_size = group_size // low_size
    position = lax.axis_index("tensor")
    high_index = position // low_size
    batch_rows = tile_rows * high_size
    seg_count = batch_rows // SEG
    row_ids = high_index * tile_rows + jnp.arange(tile_rows, dtype=jnp.int32)
    live_count = live_segment_table[0]
    keep_rows = (row_ids // SEG)[None, :] < live_count[:, None]
    masked_tile = jnp.where(keep_rows[:, :, None], grad_tile, jnp.zeros_like(grad_tile))
    gathered = masked_tile
    for level in range(low_bits, total_bits):
        received = partner(gathered, "tensor", level)
        leading = position >> level & 1 == 0
        gathered = jnp.where(
            leading,
            jnp.concatenate([gathered, received], 1),
            jnp.concatenate([received, gathered], 1),
        )
    products = jnp.einsum("mrd,id->mri", gathered, weight, preferred_element_type=jnp.float32)
    reduced = products
    for level in reversed(range(low_bits)):
        half_cols = reduced.shape[2] // 2
        lower_half = reduced[:, :, :half_cols]
        upper_half = reduced[:, :, half_cols:]
        upper_side = position >> level & 1 == 1
        kept_half = jnp.where(upper_side, upper_half, lower_half)
        sent_half = jnp.where(upper_side, lower_half, upper_half)
        reduced = kept_half + partner(sent_half, "tensor", level)
    classes = segment_adapter_class[0]
    class_indicator = (
        classes[:, :, None] == jnp.arange(up_matrix_tile.shape[0], dtype=jnp.int32)[None, None, :]
    ).astype(jnp.bfloat16)
    selected_up_matrix = choose_segment_rows(class_indicator, up_matrix_tile)
    grad_segs = gathered.reshape(micro_count, seg_count, SEG, tile_cols)
    partial_rank = jnp.einsum(
        "mskd,msrd->mskr", grad_segs, selected_up_matrix, preferred_element_type=jnp.float32
    )
    padded_rank = jnp.zeros((micro_count, seg_count, SEG, rank_extent), jnp.float32)
    padded_rank = lax.dynamic_update_slice_in_dim(
        padded_rank, partial_rank, high_index * rank_part, 3
    )
    lowrank = lax.psum(padded_rank, "tensor").astype(jnp.bfloat16)
    selected_down_matrix = choose_segment_rows(class_indicator, adapter_down_maps[0])
    adapter = jnp.einsum(
        "mskr,msrd->mskd", lowrank, selected_down_matrix, preferred_element_type=jnp.float32
    )
    input_gradient = (reduced + adapter.reshape(micro_count, batch_rows, local_portion)).astype(
        jnp.bfloat16
    )
    grad_prev = shifted(input_gradient, "pipe", -1)
    inputs_seg = forward_input[0].reshape(micro_count, seg_count, SEG, local_portion)
    segment_down_matrix = jnp.einsum(
        "mskr,mskd->msrd", lowrank, inputs_seg, preferred_element_type=jnp.float32
    )
    hidden = lax.all_gather(saved_rank_outputs[0], "tensor", axis=1, tiled=True)
    hidden_part = lax.dynamic_slice_in_dim(hidden, high_index * rank_part, rank_part, 2)
    hidden_seg = hidden_part.reshape(micro_count, seg_count, SEG, rank_part)
    segment_up_matrix = jnp.einsum(
        "mskr,mskd->msrd", hidden_seg, grad_segs, preferred_element_type=jnp.float32
    )
    wide_class_indicator = class_indicator.astype(jnp.float32)
    down_map_gradient = jnp.einsum(
        "exk,exlq->klq", wide_class_indicator, segment_down_matrix, precision=lax.Precision.HIGHEST
    ).astype(jnp.bfloat16)
    up_map_gradient = jnp.einsum(
        "exk,exlq->klq", wide_class_indicator, segment_up_matrix, precision=lax.Precision.HIGHEST
    ).astype(jnp.bfloat16)
    return (grad_prev[None], down_map_gradient[None], up_map_gradient[None, None])


def solution(mesh):
    in_specs = (
        P("pipe", "tensor", None, None, None),
        P("pipe", None, None, "tensor"),
        P("pipe", None, "tensor", None),
        P("pipe", "tensor", None, None),
        P("pipe", None, None, "tensor"),
        P("pipe", "tensor", None, None, None),
        P("pipe", None, None),
        P("pipe", None),
    )
    out_specs = (
        P("pipe", None, None, "tensor"),
        P("pipe", None, None, "tensor"),
        P("pipe", "tensor", None, None, None),
    )
    return jax.shard_map(shards, mesh=mesh, in_specs=in_specs, out_specs=out_specs, check_vma=False)
```

profile of v0, /device:TPU:9, one launch (start us, length us, event | category | flops | bytes accessed | tf_op | source)
XLA Modules:
  0.0 877.9 jit_solution(1295151885727014478)
XLA Ops:
  0.7 0.9 broadcast_compare_fusion
  1.5 1.0 bitcast_select_fusion
  2.6 3.1 collective-permute-start
  5.7 6.0 collective-permute-done
  11.8 4.7 collective-permute-start.1
  16.5 10.8 %collective-permute-done.1 = bf16[2,128,1024]{2,1,0:T(8,128)(2,1)} collective-permute-done((bf16[2,128,1024]{2,1,0:T(8,128)(2,1)S(1)}, bf16[2,128,1024]{2,1,0:T(8,128)(2,1)}, u32[]{:S(2)}, u32[]{:S(2)}) %collective-permute-start.1) | collective-permute-done | bytes 524320 | tf_op jit(solution)/shard_map/ppermute | solution.py:12
  27.3 2.1 maximum_select_fusion.1
  29.4 6.6 collective-permute-start.2
  35.9 43.0 %collective-permute-done.2 = bf16[2,256,1024]{2,1,0:T(8,128)(2,1)} collective-permute-done((bf16[2,256,1024]{2,1,0:T(8,128)(2,1)S(1)}, bf16[2,256,1024]{2,1,0:T(8,128)(2,1)}, u32[]{:S(2)}, u32[]{:S(2)}) %collective-permute-start.2) | collective-permute-done | bytes 1048608 | tf_op jit(solution)/shard_map/ppermute | solution.py:12
  78.9 2.6 maximum_select_fusion
  81.5 2.4 fusion
  83.9 2.2 slice_select_fusion
  86.7 10.6 %collective-permute-start.3 = (f32[2,512,512]{2,1,0:T(8,128)}, f32[2,512,512]{2,1,0:T(8,128)}, u32[]{:S(2)}, u32[]{:S(2)}) collective-permute-start(f32[2,512,512]{2,1,0:T(8,128)} %slice_select_fusion), channel_id=1, source_target_pairs={{0,4},{1,5},{2,6},{3,7},{4,0},{5,1},{6,2},{7,3},{8,12},{9,13},{10,... | collective-permute-start | bytes 6291464 | tf_op jit(solution)/shard_map/ppermute | solution.py:12
  97.3 272.6 %all-gather = bf16[1,2,512,64]{3,2,1,0:T(8,128)(2,1)S(1)} all-gather(bf16[1,2,8,64]{3,2,1,0:T(8,128)(2,1)S(1)} %copy-done.12), channel_id=2, replica_groups=mesh['pipe'=8,'tensor'=64] {'tensor'}, dimensions={2}, use_global_device_ids=true | all-gather | bytes 133120 | tf_op jit(solution)/shard_map/all_gather | solution.py:102
  370.0 3.6 select_add_fusion
  373.6 1.3 copy-done.3
  375.1 1.9 collective-permute-start.4
  377.2 0.9 fusion.10
  378.1 1.1 fusion.12
  379.3 2.4 convolution_dynamic-update-slice_fusion
  381.6 0.7 copy-done.7
  382.8 14.4 %collective-permute-done.4 = f32[2,512,256]{2,1,0:T(8,128)} collective-permute-done((f32[2,512,256]{2,1,0:T(8,128)S(1)}, f32[2,512,256]{2,1,0:T(8,128)}, u32[]{:S(2)}, u32[]{:S(2)}) %collective-permute-start.4) | collective-permute-done | bytes 1048608 | tf_op jit(solution)/shard_map/ppermute | solution.py:12
  397.2 1.4 select_add_fusion.1
  398.6 0.8 slice_select_fusion.2
  399.4 1.9 collective-permute-start.5
  401.9 0.7 copy.12
  402.7 374.2 %all-reduce.1 = bf16[2,4,128,64]{2,3,1,0:T(8,128)(2,1)S(1)} all-reduce(f32[2,4,128,64]{2,3,1,0:T(8,128)S(1)} %copy-done.8), channel_id=1, replica_groups=mesh['pipe'=8,'tensor'=64] {'tensor'}, use_global_device_ids=true, to_apply=%region_0.1 | all-reduce | flops 65536 | bytes 393216 | tf_op jit(solution)/shard_map/psum | solution.py:89
  776.9 1.2 fusion.9
  778.1 1.2 fusion.6
  779.3 90.0 %collective-permute-start.6 = (bf16[2,512,128]{2,1,0:T(8,128)(2,1)S(1)}, bf16[2,512,128]{2,1,0:T(8,128)(2,1)S(1)}, u32[]{:S(2)}, u32[]{:S(2)}) collective-permute-start(bf16[2,512,128]{2,1,0:T(8,128)(2,1)S(1)} %fusion.6), channel_id=1, source_target_pairs={{64,0},{128,64},{192,128},{256,192},{320,256},{384,320},{448,384},... | collective-permute-start | bytes 786440 | tf_op jit(solution)/shard_map/ppermute | solution.py:18
  870.8 6.4 collective-permute-done.6
  877.2 0.7 copy.38
  (36 shorter events, 3.5 us)
Async XLA Ops:
  0.6 80.9 %copy-start = (bf16[1,1,1024,1024]{3,2,1,0:T(8,128)(2,1)S(1)}, bf16[1,1,1024,1024]{3,2,1,0:T(8,128)(2,1)}, u32[]{:S(2)}) copy-start(bf16[1,1,1024,1024]{3,2,1,0:T(8,128)(2,1)} %param.11) | copy-start | bytes 6291460
  2.6 9.1 %collective-permute-start = (bf16[2,64,1024]{2,1,0:T(8,128)(2,1)S(1)}, bf16[2,64,1024]{2,1,0:T(8,128)(2,1)S(1)}, u32[]{:S(2)}, u32[]{:S(2)}) collective-permute-start(bf16[2,64,1024]{2,1,0:T(8,128)(2,1)S(1)} %bitcast_select_fusion), channel_id=1, source_target_pairs={{0,8},{1,9},{2,10},{3,11},{4,12},{5,13},{6,14},{7,15},{8,0},{9,1},... | collective-permute-start | bytes 786440 | tf_op jit(solution)/shard_map/ppermute | solution.py:12
  11.8 4.7 copy-start.6
  11.8 15.5 %collective-permute-start.1 = (bf16[2,128,1024]{2,1,0:T(8,128)(2,1)S(1)}, bf16[2,128,1024]{2,1,0:T(8,128)(2,1)}, u32[]{:S(2)}, u32[]{:S(2)}) collective-permute-start(bf16[2,128,1024]{2,1,0:T(8,128)(2,1)S(1)} %maximum_select_fusion.2), channel_id=1, source_target_pairs={{0,16},{1,17},{2,18},{3,19},{4,20},{5,21},{6,22},{7,23},{8,24},{9,... | collective-permute-start | bytes 1572872 | tf_op jit(solution)/shard_map/ppermute | solution.py:12
  29.4 49.6 %collective-permute-start.2 = (bf16[2,256,1024]{2,1,0:T(8,128)(2,1)S(1)}, bf16[2,256,1024]{2,1,0:T(8,128)(2,1)}, u32[]{:S(2)}, u32[]{:S(2)}) collective-permute-start(bf16[2,256,1024]{2,1,0:T(8,128)(2,1)S(1)} %maximum_select_fusion.1), channel_id=1, source_target_pairs={{0,32},{1,33},{2,34},{3,35},{4,36},{5,37},{6,38},{7,39},{8,40},{9,... | collective-permute-start | bytes 3145736 | tf_op jit(solution)/shard_map/ppermute | solution.py:12
  81.5 2.4 copy-start.1
  83.9 2.7 copy-start.5
  83.9 13.4 %copy-start.12 = (bf16[1,2,8,64]{3,2,1,0:T(8,128)(2,1)S(1)}, bf16[1,2,8,64]{3,2,1,0:T(8,128)(2,1)}, u32[]{:S(2)}) copy-start(bf16[1,2,8,64]{3,2,1,0:T(8,128)(2,1)} %param.10) | copy-start | bytes 6148
  86.7 283.3 %collective-permute-start.3 = (f32[2,512,512]{2,1,0:T(8,128)}, f32[2,512,512]{2,1,0:T(8,128)}, u32[]{:S(2)}, u32[]{:S(2)}) collective-permute-start(f32[2,512,512]{2,1,0:T(8,128)} %slice_select_fusion), channel_id=1, source_target_pairs={{0,4},{1,5},{2,6},{3,7},{4,0},{5,1},{6,2},{7,3},{8,12},{9,13},{10,... | collective-permute-start | bytes 6291464 | tf_op jit(solution)/shard_map/ppermute | solution.py:12
  373.6 1.3 copy-start.3
  374.9 2.2 copy-start.10
  374.9 2.2 copy-start.11
  375.1 22.1 %collective-permute-start.4 = (f32[2,512,256]{2,1,0:T(8,128)S(1)}, f32[2,512,256]{2,1,0:T(8,128)}, u32[]{:S(2)}, u32[]{:S(2)}) collective-permute-start(f32[2,512,256]{2,1,0:T(8,128)S(1)} %slice_select_fusion.1), channel_id=1, source_target_pairs={{0,2},{1,3},{2,0},{3,1},{4,6},{5,7},{6,4},{7,5},{8,10},{9,11},{10,... | collective-permute-start | bytes 3145736 | tf_op jit(solution)/shard_map/ppermute | solution.py:12
  377.1 5.2 copy-start.2
  379.2 17.9 %copy-start.4 = (f32[2,512,512]{2,1,0:T(8,128)S(1)}, f32[2,512,512]{2,1,0:T(8,128)}, u32[]{:S(2)}) copy-start(f32[2,512,512]{2,1,0:T(8,128)} %copy-done.3) | copy-start | bytes 6291460
  381.6 0.7 copy-start.7
  398.6 4.1 copy-start.8
  399.4 378.6 %collective-permute-start.5 = (f32[2,512,128]{2,1,0:T(8,128)}, f32[2,512,128]{2,1,0:T(8,128)}, u32[]{:S(2)}, u32[]{:S(2)}) collective-permute-start(f32[2,512,128]{2,1,0:T(8,128)} %slice_select_fusion.2), channel_id=1, source_target_pairs={{0,1},{1,0},{2,3},{3,2},{4,5},{5,4},{6,7},{7,6},{8,9},{9,8},{10,11... | collective-permute-start | bytes 1572872 | tf_op jit(solution)/shard_map/ppermute | solution.py:12
  776.9 92.5 %copy-start.9 = (bf16[1,2,512,128]{3,2,1,0:T(8,128)(2,1)S(1)}, bf16[1,2,512,128]{3,2,1,0:T(8,128)(2,1)}, u32[]{:S(2)}) copy-start(bf16[1,2,512,128]{3,2,1,0:T(8,128)(2,1)} %param.9) | copy-start | bytes 786436
  779.3 97.9 %collective-permute-start.6 = (bf16[2,512,128]{2,1,0:T(8,128)(2,1)S(1)}, bf16[2,512,128]{2,1,0:T(8,128)(2,1)S(1)}, u32[]{:S(2)}, u32[]{:S(2)}) collective-permute-start(bf16[2,512,128]{2,1,0:T(8,128)(2,1)S(1)} %fusion.6), channel_id=1, source_target_pairs={{64,0},{128,64},{192,128},{256,192},{320,256},{384,320},{448,384},... | collective-permute-start | bytes 786440 | tf_op jit(solution)/shard_map/ppermute | solution.py:18
where the time goes:
time: 878 us
  blocking collectives  647 us (74%)
  starting transfers between devices  119 us (14%)
  waiting for transfers between devices  80.5 us (9%)
  other arithmetic  16.1 us (2%)
  matrix products  9.77 us (1%)
    psum x1, blocking collectives, shards(): lowrank = lax.psum(padded_rank, 'tensor').astype(jnp.bfloat16)  374 us
    all_gather x1, blocking collectives, shards(): hidden = lax.all_gather(saved_rank_outputs[0], 'tensor', axis=1, tiled=True)  273 us
    ppermute x1, starting transfers between devices, shifted(): return lax.ppermute(block, axis, route)  90 us
    ppermute x6, waiting for transfers between devices, partner(): return lax.ppermute(value, axis, pairs)  74.1 us
    ppermute x6, starting transfers between devices, partner(): return lax.ppermute(value, axis, pairs)  28.8 us
  transfers between devices with their start and end apart: 7, of which 5 were waited for; matrix products, arithmetic and copies ran while one was open for 1% of the time, Pallas kernels for 0%

commit v1 on v0

--- a/solution.py
+++ b/solution.py
@@ -99,7 +99,12 @@
     segment_down_matrix = jnp.einsum(
         "mskr,mskd->msrd", lowrank, inputs_seg, preferred_element_type=jnp.float32
     )
-    hidden = lax.all_gather(saved_rank_outputs[0], "tensor", axis=1, tiled=True)
+    hidden = jnp.concatenate(
+        lax.all_to_all(
+            jnp.stack([saved_rank_outputs[0]] * lax.axis_size("tensor")), "tensor", 0, 0
+        ),
+        axis=1,
+    )
     hidden_part = lax.dynamic_slice_in_dim(hidden, high_index * rank_part, rank_part, 2)
     hidden_seg = hidden_part.reshape(micro_count, seg_count, SEG, rank_part)
     segment_up_matrix = jnp.einsum(

time: 878 us -> 701 us (0.80)
  the two profiles are of different devices: /device:TPU:9 before, /device:TPU:17 now
where the time goes in v1:
time: 701 us; the launch traced here: 700 us
  blocking collectives  377 us (54%)
  waiting for transfers between devices  150 us (21%)
  starting transfers between devices  140 us (20%)
  other arithmetic  16.1 us (2%)
  matrix products  9.54 us (1%)
    psum x1, blocking collectives, shards(): lowrank = lax.psum(padded_rank, 'tensor').astype(jnp.bfloat16)  377 us
    ppermute x6, waiting for transfers between devices, partner(): return lax.ppermute(value, axis, pairs)  146 us
    ppermute x6, starting transfers between devices, partner(): return lax.ppermute(value, axis, pairs)  72.5 us
    ppermute x1, starting transfers between devices, shifted(): return lax.ppermute(block, axis, route)  58.6 us
  transfers between devices with their start and end apart: 8, of which 6 were waited for; matrix products, arithmetic and copies ran while one was open for 2% of the time, Pallas kernels for 0%

profile of v1, /device:TPU:17, one launch (start us, length us, event | category | flops | bytes accessed | tf_op | source)
XLA Modules:
  0.0 700.0 jit_solution(15706163343478199111)
XLA Ops:
  0.7 0.9 broadcast_compare_fusion
  1.5 1.0 bitcast_select_fusion
  2.6 3.1 collective-permute-start
  5.7 6.0 collective-permute-done
  11.8 4.7 collective-permute-start.1
  16.5 10.8 %collective-permute-done.1 = bf16[2,128,1024]{2,1,0:T(8,128)(2,1)} collective-permute-done((bf16[2,128,1024]{2,1,0:T(8,128)(2,1)S(1)}, bf16[2,128,1024]{2,1,0:T(8,128)(2,1)}, u32[]{:S(2)}, u32[]{:S(2)}) %collective-permute-start.1) | collective-permute-done | bytes 524320 | tf_op jit(solution)/shard_map/ppermute | solution.py:12
  27.3 2.1 maximum_select_fusion.1
  29.4 5.7 collective-permute-start.2
  35.0 47.8 %collective-permute-done.2 = bf16[2,256,1024]{2,1,0:T(8,128)(2,1)} collective-permute-done((bf16[2,256,1024]{2,1,0:T(8,128)(2,1)S(1)}, bf16[2,256,1024]{2,1,0:T(8,128)(2,1)}, u32[]{:S(2)}, u32[]{:S(2)}) %collective-permute-start.2) | collective-permute-done | bytes 1048608 | tf_op jit(solution)/shard_map/ppermute | solution.py:12
  82.8 2.6 maximum_select_fusion
  85.4 2.4 fusion
  87.9 2.2 slice_select_fusion
  90.6 10.6 %collective-permute-start.3 = (f32[2,512,512]{2,1,0:T(8,128)}, f32[2,512,512]{2,1,0:T(8,128)}, u32[]{:S(2)}, u32[]{:S(2)}) collective-permute-start(f32[2,512,512]{2,1,0:T(8,128)} %slice_select_fusion), channel_id=1, source_target_pairs={{0,4},{1,5},{2,6},{3,7},{4,0},{5,1},{6,2},{7,3},{8,12},{9,13},{10,... | collective-permute-start | bytes 6291464 | tf_op jit(solution)/shard_map/ppermute | solution.py:12
  101.2 0.8 reshape.85
  102.1 9.3 %all-to-all-start = ((bf16[64,2,512]{2,1,0:T(2,128)(2,1)}), bf16[64,2,512]{2,1,0:T(2,128)(2,1)S(1)}, u32[]{:S(2)}, u32[]{:S(2)}) async-start(bf16[64,2,512]{2,1,0:T(2,128)(2,1)} %reshape.85), calls=%async_computation | async-start | bytes 262144 | tf_op jit(solution)/shard_map/all_to_all | solution.py:103
  111.5 0.9 convolution_convert_fusion
  112.4 40.1 %collective-permute-done.3 = f32[2,512,512]{2,1,0:T(8,128)} collective-permute-done((f32[2,512,512]{2,1,0:T(8,128)}, f32[2,512,512]{2,1,0:T(8,128)}, u32[]{:S(2)}, u32[]{:S(2)}) %collective-permute-start.3) | collective-permute-done | bytes 2097184 | tf_op jit(solution)/shard_map/ppermute | solution.py:12
  152.4 3.6 select_add_fusion
  156.0 1.3 copy-done.3
  157.5 46.5 %collective-permute-start.4 = (f32[2,512,256]{2,1,0:T(8,128)S(1)}, f32[2,512,256]{2,1,0:T(8,128)}, u32[]{:S(2)}, u32[]{:S(2)}) collective-permute-start(f32[2,512,256]{2,1,0:T(8,128)S(1)} %slice_select_fusion.1), channel_id=1, source_target_pairs={{0,2},{1,3},{2,0},{3,1},{4,6},{5,7},{6,4},{7,5},{8,10},{9,11},{10,... | collective-permute-start | bytes 3145736 | tf_op jit(solution)/shard_map/ppermute | solution.py:12
  204.0 0.9 convolution_convert_fusion.1
  205.4 2.4 convolution_dynamic-update-slice_fusion
  208.2 41.8 %collective-permute-done.4 = f32[2,512,256]{2,1,0:T(8,128)} collective-permute-done((f32[2,512,256]{2,1,0:T(8,128)S(1)}, f32[2,512,256]{2,1,0:T(8,128)}, u32[]{:S(2)}, u32[]{:S(2)}) %collective-permute-start.4) | collective-permute-done | bytes 1048608 | tf_op jit(solution)/shard_map/ppermute | solution.py:12
  250.1 1.4 select_add_fusion.1
  251.5 0.9 slice_select_fusion.2
  252.4 1.9 collective-permute-start.5
  254.8 0.7 copy.33
  255.6 377.3 %all-reduce.1 = bf16[2,4,128,64]{2,3,1,0:T(8,128)(2,1)S(1)} all-reduce(f32[2,4,128,64]{2,3,1,0:T(8,128)S(1)} %convolution_dynamic-update-slice_fusion), channel_id=1, replica_groups=mesh['pipe'=8,'tensor'=64] {'tensor'}, use_global_device_ids=true, to_apply=%region_0.1 | all-reduce | flops 65536 | bytes 393216 | tf_op jit(solution)/shard_map/psum | solution.py:89
  632.9 1.2 fusion.11
  634.1 1.2 fusion.6
  635.3 58.6 %collective-permute-start.6 = (bf16[2,512,128]{2,1,0:T(8,128)(2,1)S(1)}, bf16[2,512,128]{2,1,0:T(8,128)(2,1)S(1)}, u32[]{:S(2)}, u32[]{:S(2)}) collective-permute-start(bf16[2,512,128]{2,1,0:T(8,128)(2,1)S(1)} %fusion.6), channel_id=1, source_target_pairs={{64,0},{128,64},{192,128},{256,192},{320,256},{384,320},{448,384},... | collective-permute-start | bytes 786440 | tf_op jit(solution)/shard_map/ppermute | solution.py:18
  695.4 3.9 collective-permute-done.6
  (39 shorter events, 4.4 us)
Async XLA Ops:
  0.6 84.8 %copy-start = (bf16[1,1,1024,1024]{3,2,1,0:T(8,128)(2,1)S(1)}, bf16[1,1,1024,1024]{3,2,1,0:T(8,128)(2,1)}, u32[]{:S(2)}) copy-start(bf16[1,1,1024,1024]{3,2,1,0:T(8,128)(2,1)} %param.11) | copy-start | bytes 6291460
  2.6 9.1 %collective-permute-start = (bf16[2,64,1024]{2,1,0:T(8,128)(2,1)S(1)}, bf16[2,64,1024]{2,1,0:T(8,128)(2,1)S(1)}, u32[]{:S(2)}, u32[]{:S(2)}) collective-permute-start(bf16[2,64,1024]{2,1,0:T(8,128)(2,1)S(1)} %bitcast_select_fusion), channel_id=1, source_target_pairs={{0,8},{1,9},{2,10},{3,11},{4,12},{5,13},{6,14},{7,15},{8,0},{9,1},... | collective-permute-start | bytes 786440 | tf_op jit(solution)/shard_map/ppermute | solution.py:12
  11.8 4.7 copy-start.6
  11.8 15.5 %collective-permute-start.1 = (bf16[2,128,1024]{2,1,0:T(8,128)(2,1)S(1)}, bf16[2,128,1024]{2,1,0:T(8,128)(2,1)}, u32[]{:S(2)}, u32[]{:S(2)}) collective-permute-start(bf16[2,128,1024]{2,1,0:T(8,128)(2,1)S(1)} %maximum_select_fusion.2), channel_id=1, source_target_pairs={{0,16},{1,17},{2,18},{3,19},{4,20},{5,21},{6,22},{7,23},{8,24},{9,... | collective-permute-start | bytes 1572872 | tf_op jit(solution)/shard_map/ppermute | solution.py:12
  29.4 53.4 %collective-permute-start.2 = (bf16[2,256,1024]{2,1,0:T(8,128)(2,1)S(1)}, bf16[2,256,1024]{2,1,0:T(8,128)(2,1)}, u32[]{:S(2)}, u32[]{:S(2)}) collective-permute-start(bf16[2,256,1024]{2,1,0:T(8,128)(2,1)S(1)} %maximum_select_fusion.1), channel_id=1, source_target_pairs={{0,32},{1,33},{2,34},{3,35},{4,36},{5,37},{6,38},{7,39},{8,40},{9,... | collective-permute-start | bytes 3145736 | tf_op jit(solution)/shard_map/ppermute | solution.py:12
  85.4 2.4 copy-start.1
  87.8 2.8 copy-start.5
  87.8 13.4 %copy-start.11 = (bf16[1,2,8,64]{3,2,1,0:T(8,128)(2,1)S(1)}, bf16[1,2,8,64]{3,2,1,0:T(8,128)(2,1)}, u32[]{:S(2)}) copy-start(bf16[1,2,8,64]{3,2,1,0:T(8,128)(2,1)} %param.10) | copy-start | bytes 6148
  87.8 23.6 %copy-start.8 = (bf16[1,8,64,128]{3,2,1,0:T(8,128)(2,1)S(1)}, bf16[1,8,64,128]{3,2,1,0:T(8,128)(2,1)}, u32[]{:S(2)}) copy-start(bf16[1,8,64,128]{3,2,1,0:T(8,128)(2,1)} %param.12) | copy-start | bytes 393220
  87.8 23.6 %copy-start.10 = (s32[1,2,4]{2,1,0:T(2,128)S(1)}, s32[1,2,4]{2,1,0:T(2,128)}, u32[]{:S(2)}) copy-start(s32[1,2,4]{2,1,0:T(2,128)} %param.14) | copy-start | bytes 100
  90.6 61.9 %collective-permute-start.3 = (f32[2,512,512]{2,1,0:T(8,128)}, f32[2,512,512]{2,1,0:T(8,128)}, u32[]{:S(2)}, u32[]{:S(2)}) collective-permute-start(f32[2,512,512]{2,1,0:T(8,128)} %slice_select_fusion), channel_id=1, source_target_pairs={{0,4},{1,5},{2,6},{3,7},{4,0},{5,1},{6,2},{7,3},{8,12},{9,13},{10,... | collective-permute-start | bytes 6291464 | tf_op jit(solution)/shard_map/ppermute | solution.py:12
  102.1 102.9 %all-to-all-start = ((bf16[64,2,512]{2,1,0:T(2,128)(2,1)}), bf16[64,2,512]{2,1,0:T(2,128)(2,1)S(1)}, u32[]{:S(2)}, u32[]{:S(2)}) async-start(bf16[64,2,512]{2,1,0:T(2,128)(2,1)} %reshape.85), calls=%async_computation | async-start | bytes 262144 | tf_op jit(solution)/shard_map/all_to_all | solution.py:103
  156.0 1.3 copy-start.3
  157.4 46.7 %copy-start.9 = (bf16[1,1,8,8,1024]{4,3,2,1,0:T(8,128)(2,1)S(1)}, bf16[1,1,8,8,1024]{4,3,2,1,0:T(8,128)(2,1)}, u32[]{:S(2)}) copy-start(bf16[1,1,8,8,1024]{4,3,2,1,0:T(8,128)(2,1)} %param.13) | copy-start | bytes 393220
  157.5 92.5 %collective-permute-start.4 = (f32[2,512,256]{2,1,0:T(8,128)S(1)}, f32[2,512,256]{2,1,0:T(8,128)}, u32[]{:S(2)}, u32[]{:S(2)}) collective-permute-start(f32[2,512,256]{2,1,0:T(8,128)S(1)} %slice_select_fusion.1), channel_id=1, source_target_pairs={{0,2},{1,3},{2,0},{3,1},{4,6},{5,7},{6,4},{7,5},{8,10},{9,11},{10,... | collective-permute-start | bytes 3145736 | tf_op jit(solution)/shard_map/ppermute | solution.py:12
  205.2 2.6 copy-start.2
  205.4 44.7 %copy-start.4 = (f32[2,512,512]{2,1,0:T(8,128)S(1)}, f32[2,512,512]{2,1,0:T(8,128)}, u32[]{:S(2)}) copy-start(f32[2,512,512]{2,1,0:T(8,128)} %copy-done.3) | copy-start | bytes 6291460
  252.4 381.8 %collective-permute-start.5 = (f32[2,512,128]{2,1,0:T(8,128)}, f32[2,512,128]{2,1,0:T(8,128)}, u32[]{:S(2)}, u32[]{:S(2)}) collective-permute-start(f32[2,512,128]{2,1,0:T(8,128)} %slice_select_fusion.2), channel_id=1, source_target_pairs={{0,1},{1,0},{2,3},{3,2},{4,5},{5,4},{6,7},{7,6},{8,9},{9,8},{10,11... | collective-permute-start | bytes 1572872 | tf_op jit(solution)/shard_map/ppermute | solution.py:12
  632.9 61.0 %copy-start.7 = (bf16[1,2,512,128]{3,2,1,0:T(8,128)(2,1)S(1)}, bf16[1,2,512,128]{3,2,1,0:T(8,128)(2,1)}, u32[]{:S(2)}) copy-start(bf16[1,2,512,128]{3,2,1,0:T(8,128)(2,1)} %param.9) | copy-start | bytes 786436
  635.3 64.0 %collective-permute-start.6 = (bf16[2,512,128]{2,1,0:T(8,128)(2,1)S(1)}, bf16[2,512,128]{2,1,0:T(8,128)(2,1)S(1)}, u32[]{:S(2)}, u32[]{:S(2)}) collective-permute-start(bf16[2,512,128]{2,1,0:T(8,128)(2,1)S(1)} %fusion.6), channel_id=1, source_target_pairs={{64,0},{128,64},{192,128},{256,192},{320,256},{384,320},{448,384},... | collective-permute-start | bytes 786440 | tf_op jit(solution)/shard_map/ppermute | solution.py:18
